TPU v7x, 32 devices: a whole 2x2x4 slice. The times are simulated.
32 devices in a mesh: ex: 8 (over y, x, core), feat: 4 (over z).
Axes of the slice: x: 2, y: 2, z: 4, core: 2. Of those that a mesh axis runs over, the one named last changes fastest.
Arguments:
- activations: bfloat16 [512, 64, 4096], P('ex', None, 'feat'), may hold values from -6 to 6
- output_gradient_rows: bfloat16 [512, 64, 4096], P('ex', None, 'feat'), may hold values from -6 to 6
- adapter_down_matrix: bfloat16 [4096, 128], P('feat'), may hold values from -0.09375 to 0.09375
- rank_side_sketch: bfloat16 [128, 64], replicated, may hold values from -0.5 to 0.5
- output_side_sketch: bfloat16 [4096, 128], P('feat'), may hold values from -0.09375 to 0.09375
- heldout_gradient_features: float32 [256, 8192], P('ex', 'feat'), may hold values from -6 to 6
- heldout_language_permutation: int32 [256], P('ex'), may hold values from 0 to 255, each once
Outputs:
- scores: float32 [512, 64], P('ex')
Inputs may be any that keep to these rules, and one draw needn't show every extreme that they name: `heldout_language_permutation`: every value of 0 to 255 appears once, so every language has 4 validation examples.
All inputs are finite; a program needn't handle non-finite values.
Results may differ from a plain program's by a relative error of at most 0.0029.
Values sent between devices are 32-bit elements; how exact they have to be, the bound alone decides.
No kernel may reach another device: no remote copies, remote signals or barrier semaphores. Data moves between devices by JAX's collectives and lax.ppermute only.
A program may use at most 64 MiB of HBM per device.

v0:
```python
import jax
import jax.numpy as jnp
from jax import lax
from jax.sharding import PartitionSpec as P

KF = 8192
LANGS = 64


def shards(
    activations,
    output_gradient_rows,
    adapter_down_matrix,
    rank_side_sketch,
    output_side_sketch,
    heldout_gradient_features,
    heldout_language_permutation,
):
    highest = lax.Precision.HIGHEST
    ex_dev = activations.shape[0]
    down_projection_name = jnp.dot(
        adapter_down_matrix, rank_side_sketch, preferred_element_type=jnp.float32
    ).astype(jnp.bfloat16)
    rank_part = jnp.einsum(
        "esd,dr->esr", activations, down_projection_name, preferred_element_type=jnp.float32
    )
    rank_side = lax.psum(rank_part, "feat")
    out_part = jnp.einsum(
        "esd,dk->esk", output_gradient_rows, output_side_sketch, preferred_element_type=jnp.float32
    )
    out_side = lax.psum_scatter(out_part, "feat", scatter_dimension=2, tiled=True)
    grad_feat = jnp.einsum("esk,esr->ekr", out_side, rank_side, precision=highest).reshape(
        ex_dev, -1
    )
    val_square = lax.psum(
        jnp.sum(heldout_gradient_features * heldout_gradient_features, axis=1), "feat"
    )
    val_unit = heldout_gradient_features * lax.rsqrt(val_square + 1e-06)[:, None]
    lang = heldout_language_permutation % LANGS
    onehot = (lang[:, None] == jnp.arange(LANGS, dtype=jnp.int32)[None, :]).astype(jnp.float32)
    lang_part = jnp.dot(onehot.T, val_unit, precision=highest)
    lang_mean = lax.psum(lang_part, "ex") / (
        heldout_language_permutation.shape[0] * lax.axis_size("ex") // LANGS
    )
    inner_part = jnp.dot(grad_feat, lang_mean.T, precision=highest)
    square_part = jnp.sum(grad_feat * grad_feat, axis=1)
    inner, squares = lax.psum((inner_part, square_part), "feat")
    per_lang = heldout_language_permutation.shape[0] * lax.axis_size("ex") // LANGS
    scale = jnp.sqrt(jnp.float32(KF * per_lang))
    return scale * inner * lax.rsqrt(squares + 1e-06)[:, None]


def solution(mesh):
    placed = (
        P("ex", None, "feat"),
        P("ex", None, "feat"),
        P("feat", None),
        P(),
        P("feat", None),
        P("ex", "feat"),
        P("ex"),
    )
    return jax.shard_map(
        shards, mesh=mesh, in_specs=placed, out_specs=P("ex", None), check_vma=False
    )
```

profile of v0, /device:TPU:0, one launch (start us, length us, event | category | flops | bytes accessed | tf_op | source)
XLA Modules:
  0.0 268.0 jit_solution(1419638174889042181)
XLA Ops:
  6.5 0.0 copy-start
  6.5 0.0 all-reduce.4.cloned.1.call-start
  6.5 7.4 %convolution_bitcast_fusion = f32[64,64,64]{2,1,0:T(8,128)} fusion(bf16[64,64,1024]{2,1,0:T(8,128)(2,1)} %param.7, bf16[1024,128]{1,0:T(8,128)(2,1)} %param.9, bf16[128,64]{0,1:T(8,128)(2,1)} %param.10), kind=kOutput, calls=%fused_computation | convolution fusion | flops 553713664 | bytes 9715712 | tf_op jit(solution)/shard_map/esd,dr->esr/dot_general | solution.py:24
  14.0 0.0 all-reduce.4.cloned.1.call-update
  14.0 0.0 copy-start.1
  14.0 0.0 copy-start.2
  14.0 0.0 reduce-scatter.2.cloned.1.call-start
  14.1 0.0 copy-done
  14.1 9.5 %fusion.3 = f32[64,64,128]{1,2,0:T(8,128)} fusion(bf16[64,64,1024]{2,1,0:T(8,128)(2,1)} %param.8, bf16[1024,128]{1,0:T(8,128)(2,1)S(1)} %copy-done), kind=kOutput, calls=%fused_computation.6 | convolution fusion | flops 1073741824 | bytes 10747904 | tf_op jit(solution)/shard_map/esd,dk->esk/dot_general | solution.py:28
  23.5 0.0 reduce-scatter.2.cloned.1.call-update
  23.6 0.0 all-reduce.6.cloned.1.call-start
  23.6 0.0 copy-done.1
  23.6 0.1 multiply_reduce_fusion.1
  23.7 14.1 %psum.36 = f32[32]{0:T(128)S(1)} all-reduce(f32[32]{0:T(128)S(1)} %multiply_reduce_fusion.1), channel_id=1, replica_groups=mesh['ex'=8,'feat'=4] {'feat'}, use_global_device_ids=true, to_apply=%region_3.0 | all-reduce | flops 32 | bytes 256 | tf_op jit(solution)/shard_map/psum | solution.py:35
  37.8 1.3 fusion.6
  39.1 0.0 all-reduce.6.cloned.1.call-update
  39.1 64.1 %all-reduce.4.cloned.1.call-done = f32[64,64,64]{2,1,0:T(8,128)} async-done(((f32[64,64,64]{2,1,0:T(8,128)}), f32[64,64,64]{2,1,0:T(8,128)}) %all-reduce.4.cloned.1.call-update) | async-done | bytes 1048592 | tf_op jit(solution)/shard_map/psum | solution.py:27
  103.3 78.1 %reduce-scatter.2.cloned.1.call-done = f32[64,64,32]{1,2,0:T(8,128)} async-done(((f32[64,64,128]{1,2,0:T(8,128)}), f32[64,64,32]{1,2,0:T(8,128)}) %reduce-scatter.2.cloned.1.call-update) | async-done | bytes 524304 | tf_op jit(solution)/shard_map/reduce_scatter | solution.py:31
  181.4 4.2 %multiply_reduce_fusion = (f32[64]{0:T(128)S(1)}, f32[64,32,64]{2,1,0:T(8,128)S(1)}) fusion(f32[64,64,32]{1,2,0:T(8,128)} %reduce-scatter.2.cloned.1.call-done, f32[64,64,64]{2,1,0:T(8,128)} %all-reduce.4.cloned.1.call-done), kind=kOutput, calls=%fused_computation.3 | convolution fusion | flops 100925376 | bytes 2097408 | tf_op jit(solution)/shard_map/esk,esr->ekr/dot_general | solution.py:32
  185.6 0.4 reshape.6
  186.0 53.9 %all-reduce.6.cloned.1.call-done = f32[64,2048]{1,0:T(8,128)} async-done(((f32[64,2048]{1,0:T(8,128)}), f32[64,2048]{1,0:T(8,128)}) %all-reduce.6.cloned.1.call-update) | async-done | bytes 524304 | tf_op jit(solution)/shard_map/psum | solution.py:42
  239.9 1.6 fusion.1
  241.5 19.3 %all-reduce = (f32[64,64]{1,0:T(8,128)S(1)}, f32[64]{0:T(128)S(1)}) all-reduce(f32[64,64]{1,0:T(8,128)S(1)} %fusion.1, f32[64]{0:T(128)S(1)} %get-tuple-element.7), channel_id=1, replica_groups=mesh['ex'=8,'feat'=4] {'feat'}, use_global_device_ids=true, to_apply=%region_5.6 | all-reduce | flops 4160 | bytes 33280 | tf_op jit(solution)/shard_map/psum | solution.py:47
  260.8 0.7 broadcast_multiply_fusion
  (4 shorter events, 0.0 us)
Async XLA Ops:
  6.5 7.5 %copy-start = (bf16[1024,128]{1,0:T(8,128)(2,1)S(1)}, bf16[1024,128]{1,0:T(8,128)(2,1)}, u32[]{:S(2)}) copy-start(bf16[1024,128]{1,0:T(8,128)(2,1)} %param.11) | copy-start | bytes 786436
  6.5 96.7 %all-reduce.4.cloned.1.call-start = ((), (), s32[]{:S(2)}) async-start(), calls=%async_computation.2 | async-start | bytes 4194304 | tf_op jit(solution)/shard_map/psum | solution.py:27
  14.0 9.6 %copy-start.1 = (f32[32,2048]{1,0:T(8,128)S(1)}, f32[32,2048]{1,0:T(8,128)}, u32[]{:S(2)}) copy-start(f32[32,2048]{1,0:T(8,128)} %param.12) | copy-start | bytes 786436
  14.0 23.8 %copy-start.2 = (s32[32]{0:T(128)S(1)}, s32[32]{0:T(128)}, u32[]{:S(2)}) copy-start(s32[32]{0:T(128)} %param.13) | copy-start | bytes 388
  14.0 167.4 %reduce-scatter.2.cloned.1.call-start = ((), (), s32[]{:S(2)}) async-start(), calls=%async_computation.1 | async-start | bytes 5242880 | tf_op jit(solution)/shard_map/reduce_scatter | solution.py:31
  23.6 216.3 %all-reduce.6.cloned.1.call-start = ((), (), s32[]{:S(2)}) async-start(), calls=%async_computation.3 | async-start | bytes 1048576 | tf_op jit(solution)/shard_map/psum | solution.py:42
Sparse Core Ops, SparseCore 0:
  14.1 89.1 all-reduce.3
  105.6 75.8 reduce-scatter.1
  184.5 55.3 all-reduce.5
where the time goes:
time: 268 us
  waiting for transfers between devices  196 us (73%)
  blocking collectives  33.3 us (12%)
  matrix products  23.9 us (9%)
  between operations  13.2 us (5%)
    reduce_scatter x1, waiting for transfers between devices, shards(): lax.psum_scatter(out_part, 'feat', scatter_dimension=2, tiled=True)  78.1 us
    psum x1, waiting for transfers between devices, shards(): rank_side = lax.psum(rank_part, 'feat')  64.1 us
    psum x1, waiting for transfers between devices, shards(): lax.psum(lang_part, 'ex')  53.9 us
    psum x1, blocking collectives, shards(): inner, squares = lax.psum((inner_part, square_part), 'feat')  19.3 us
    psum x1, blocking collectives, shards(): lax.psum(jnp.sum(heldout_gradient_features * heldout_gradient_features, a...  14.1 us
    dot_general x1, matrix products, shards(): jnp.einsum('esd,dk->esk', output_gradient_rows, output_side_sketch, prefe...  9.45 us
    dot_general x1, matrix products, shards(): jnp.einsum('esd,dr->esr', activations, down_projection_name, preferred_el...  7.42 us
  transfers between devices with their start and end apart: 3, of which 3 were waited for; matrix products, arithmetic and copies ran while one was open for 6% of the time, Pallas kernels for 0%

commit v1 on v0

--- a/solution.py
+++ b/solution.py
@@ -24,7 +24,20 @@
     rank_part = jnp.einsum(
         "esd,dr->esr", activations, down_projection_name, preferred_element_type=jnp.float32
     )
-    rank_side = lax.psum(rank_part, "feat")
+
+    def frame_direct(sheet):
+        n_peers_all = lax.axis_size("feat")
+        item_now = sheet
+        for b in [
+            [(at, at ^ ix) for at in range(n_peers_all)]
+            for ix in (1, 2, 4, 8, 16)
+            if ix < n_peers_all
+        ]:
+            near = lax.ppermute(item_now, "feat", b)
+            item_now = item_now + near
+        return item_now
+
+    rank_side = frame_direct(rank_part)
     out_part = jnp.einsum(
         "esd,dk->esk", output_gradient_rows, output_side_sketch, preferred_element_type=jnp.float32
     )

time: 268 us -> 322 us (1.20)
  blocking collectives: 33.3 us -> 70.6 us
  waiting for transfers between devices: 196 us -> 202 us
    ppermute x0 -> x2, waiting for transfers between devices: none -> 152 us  [frame_direct(): near = lax.ppermute(item_now, 'feat', b)]
    reduce_scatter x1, waiting for transfers between devices: 78.1 us -> 0.01 us  [shards(): lax.psum_scatter(out_part, 'feat', scatter_dimension=2, tiled=True)]
    psum x1 -> x0, waiting for transfers between devices: 64.1 us -> none  [shards(): rank_side = lax.psum(rank_part, 'feat')]
    psum x1, blocking collectives: 14.1 us -> 51.3 us  [shards(): lax.psum(jnp.sum(heldout_gradient_features * heldout_gradient_features, a...]
    psum x1, waiting for transfers between devices: 53.9 us -> 50.1 us  [shards(): lax.psum(lang_part, 'ex')]
  transfers between devices with their start and end apart: 3 -> 4, of which waited for: 3 -> 3; matrix products, arithmetic and copies ran while one was open for 6% -> 5% of each run, Pallas kernels for 0% -> 0%
where the time goes in v1:
time: 322 us
  waiting for transfers between devices  202 us (63%)
  blocking collectives  70.6 us (22%)
  matrix products  25.4 us (8%)
  between operations  14.9 us (5%)
  starting transfers between devices  3.23 us (1%)
    ppermute x2, waiting for transfers between devices, frame_direct(): near = lax.ppermute(item_now, 'feat', b)  152 us
    psum x1, blocking collectives, shards(): lax.psum(jnp.sum(heldout_gradient_features * heldout_gradient_features, a...  51.3 us
    psum x1, waiting for transfers between devices, shards(): lax.psum(lang_part, 'ex')  50.1 us
    psum x1, blocking collectives, shards(): inner, squares = lax.psum((inner_part, square_part), 'feat')  19.3 us
    dot_general x1, matrix products, shards(): jnp.einsum('esd,dk->esk', output_gradient_rows, output_side_sketch, prefe...  9.44 us
    dot_general x1, matrix products, shards(): jnp.einsum('esd,dr->esr', activations, down_projection_name, preferred_el...  7.58 us
  transfers between devices with their start and end apart: 4, of which 3 were waited for; matrix products, arithmetic and copies ran while one was open for 5% of the time, Pallas kernels for 0%

profile of v1, /device:TPU:0, one launch (start us, length us, event | category | flops | bytes accessed | tf_op | source)
XLA Modules:
  0.0 321.6 jit_solution(12498878128094886975)
XLA Ops:
  7.4 0.9 copy-done
  8.3 9.4 %fusion.5 = f32[64,64,128]{1,2,0:T(8,128)} fusion(bf16[64,64,1024]{2,1,0:T(8,128)(2,1)} %param.8, bf16[1024,128]{1,0:T(8,128)(2,1)S(1)} %copy-done), kind=kOutput, calls=%fused_computation.8 | convolution fusion | flops 1073741824 | bytes 10747904 | tf_op jit(solution)/shard_map/esd,dk->esk/dot_general | solution.py:41
  17.8 0.0 reduce-scatter.2.cloned.1.call-update
  17.8 0.0 all-reduce.3.cloned.1.call-start
  17.8 0.9 copy-done.3
  18.7 7.6 %convolution_bitcast_fusion = f32[64,64,64]{1,2,0:T(8,128)S(1)} fusion(bf16[64,64,1024]{2,1,0:T(8,128)(2,1)} %param.7, bf16[1024,128]{1,0:T(8,128)(2,1)S(1)} %copy-done.3, bf16[128,64]{0,1:T(8,128)(2,1)S(1)} %copy-done.4), kind=kOutput, calls=%fused_computation.2 | convolution fusion | flops 553713664 | bytes 9715712 | tf_op jit(solution)/shard_map/esd,dr->esr/dot_general | solution.py:24
  26.3 0.0 copy-start.2
  26.3 0.0 copy-start.5
  26.3 3.1 collective-permute-start
  29.4 0.0 copy-done.1
  29.4 111.5 %collective-permute-done = f32[64,64,64]{1,2,0:T(8,128)S(1)} collective-permute-done((f32[64,64,64]{1,2,0:T(8,128)S(1)}, f32[64,64,64]{1,2,0:T(8,128)S(1)}, u32[]{:S(2)}, u32[]{:S(2)}) %collective-permute-start) | collective-permute-done | bytes 1048608 | tf_op jit(solution)/shard_map/ppermute | solution.py:36
  141.0 2.1 add.34
  143.0 0.1 collective-permute-start.1
  143.1 0.1 multiply_reduce_fusion.1
  143.2 51.3 %psum.28 = f32[32]{0:T(128)S(1)} all-reduce(f32[32]{0:T(128)S(1)} %multiply_reduce_fusion.1), channel_id=1, replica_groups=mesh['ex'=8,'feat'=4] {'feat'}, use_global_device_ids=true, to_apply=%region_2.0 | all-reduce | flops 32 | bytes 256 | tf_op jit(solution)/shard_map/psum | solution.py:48
  194.6 1.3 fusion.8
  195.9 0.0 all-reduce.3.cloned.1.call-update
  195.9 40.7 %collective-permute-done.1 = f32[64,64,64]{1,2,0:T(8,128)} collective-permute-done((f32[64,64,64]{1,2,0:T(8,128)S(1)}, f32[64,64,64]{1,2,0:T(8,128)}, u32[]{:S(2)}, u32[]{:S(2)}) %collective-permute-start.1) | collective-permute-done | bytes 1048608 | tf_op jit(solution)/shard_map/ppermute | solution.py:36
  236.6 5.5 %multiply_reduce_fusion = (f32[64]{0:T(128)S(1)}, f32[64,32,64]{2,1,0:T(8,128)S(1)}) fusion(f32[64,64,32]{1,2,0:T(8,128)} %reduce-scatter.2.cloned.1.call-done, f32[64,64,64]{1,2,0:T(8,128)S(1)} %add.34, f32[64,64,64]{1,2,0:T(8,128)} %collective-permute-done.1), kind=kOutput, calls=%fused_computation.5 | convolution fusion | flops 101187520 | bytes 3145984 | tf_op jit(solution)/shard_map/esk,esr->ekr/dot_general | solution.py:45
  242.0 0.4 reshape.6
  242.4 50.1 %all-reduce.3.cloned.1.call-done = f32[64,2048]{1,0:T(8,128)} async-done(((f32[64,2048]{1,0:T(8,128)}), f32[64,2048]{1,0:T(8,128)}) %all-reduce.3.cloned.1.call-update) | async-done | bytes 524304 | tf_op jit(solution)/shard_map/psum | solution.py:55
  292.5 1.6 fusion.3
  294.1 19.3 %all-reduce = (f32[64,64]{1,0:T(8,128)S(1)}, f32[64]{0:T(128)S(1)}) all-reduce(f32[64,64]{1,0:T(8,128)S(1)} %fusion.3, f32[64]{0:T(128)S(1)} %get-tuple-element.7), channel_id=1, replica_groups=mesh['ex'=8,'feat'=4] {'feat'}, use_global_device_ids=true, to_apply=%region_4.5 | all-reduce | flops 4160 | bytes 33280 | tf_op jit(solution)/shard_map/psum | solution.py:60
  313.4 0.7 broadcast_multiply_fusion
  (12 shorter events, 0.0 us)
Async XLA Ops:
  7.4 1.0 copy-start
  7.4 229.2 %reduce-scatter.2.cloned.1.call-start = ((), (), s32[]{:S(2)}) async-start(), calls=%async_computation.1 | async-start | bytes 5242880 | tf_op jit(solution)/shard_map/reduce_scatter | solution.py:44
  17.8 0.9 copy-start.3
  17.8 1.0 copy-start.4
  17.8 274.7 %all-reduce.3.cloned.1.call-start = ((), (), s32[]{:S(2)}) async-start(), calls=%async_computation.2 | async-start | bytes 1048576 | tf_op jit(solution)/shard_map/psum | solution.py:55
  26.3 3.2 copy-start.1
  26.3 116.8 %copy-start.2 = (f32[32,2048]{1,0:T(8,128)S(1)}, f32[32,2048]{1,0:T(8,128)}, u32[]{:S(2)}) copy-start(f32[32,2048]{1,0:T(8,128)} %param.12) | copy-start | bytes 786436
  26.3 168.3 %copy-start.5 = (s32[32]{0:T(128)S(1)}, s32[32]{0:T(128)}, u32[]{:S(2)}) copy-start(s32[32]{0:T(128)} %param.13) | copy-start | bytes 388
  26.3 114.6 %collective-permute-start = (f32[64,64,64]{1,2,0:T(8,128)S(1)}, f32[64,64,64]{1,2,0:T(8,128)S(1)}, u32[]{:S(2)}, u32[]{:S(2)}) collective-permute-start(f32[64,64,64]{1,2,0:T(8,128)S(1)} %convolution_bitcast_fusion), channel_id=1, source_target_pairs={{0,1},{1,0},{2,3},{3,2},{4,5},{5,4},{6,7},{7,6},{8,9},{9,8},{10,11... | collective-permute-start | bytes 3145736 | tf_op jit(solution)/shard_map/ppermute | solution.py:36
  143.0 93.5 %collective-permute-start.1 = (f32[64,64,64]{1,2,0:T(8,128)S(1)}, f32[64,64,64]{1,2,0:T(8,128)}, u32[]{:S(2)}, u32[]{:S(2)}) collective-permute-start(f32[64,64,64]{1,2,0:T(8,128)S(1)} %add.34), channel_id=1, source_target_pairs={{0,2},{1,3},{2,0},{3,1},{4,6},{5,7},{6,4},{7,5},{8,10},{9,11},{10,... | collective-permute-start | bytes 3145736 | tf_op jit(solution)/shard_map/ppermute | solution.py:36
Sparse Core Ops, SparseCore 0:
  17.9 123.8 reduce-scatter.1
Sparse Core Ops, SparseCore 1:
  196.0 96.5 all-reduce.2
